TPU v7x, 32 devices: a whole 2x2x4 slice. The times are simulated.
32 devices in a mesh: dp: 16 (over z, y, core), tensor: 2 (over x).
Axes of the slice: x: 2, y: 2, z: 4, core: 2. Of those that a mesh axis runs over, the one named last changes fastest.
Arguments:
- block_input: bfloat16 [32768, 1024], P(('dp', 'tensor')), may hold values from -6 to 6
- mixer_gain: float32 [1024], replicated, may hold values from 0.25 to 1.75
- in_weight: bfloat16 [1024, 3, 1024], P(None, None, 'tensor'), may hold values from -0.1875 to 0.1875
- conv_kernel: bfloat16 [3, 1024], P(None, 'tensor'), may hold values from -3.5 to 3.5
- out_weight: bfloat16 [1024, 1024], P('tensor'), may hold values from -0.1875 to 0.1875
- ffn_gain: float32 [1024], replicated, may hold values from 0.25 to 1.75
- gate_weight: bfloat16 [1024, 4608], P(None, 'tensor'), may hold values from -0.1875 to 0.1875
- up_weight: bfloat16 [1024, 4608], P(None, 'tensor'), may hold values from -0.1875 to 0.1875
- down_weight: bfloat16 [4608, 1024], P('tensor'), may hold values from -0.09375 to 0.09375
- output_grad: bfloat16 [32768, 1024], P(('dp', 'tensor')), may hold values from -6 to 6
- lengths: int32 [32], P('dp'), may hold values from 256 to 1024, as said below
Outputs:
- block_output: bfloat16 [32768, 1024], P(('dp', 'tensor'))
- input_grad: bfloat16 [32768, 1024], P(('dp', 'tensor'))
- mixer_gain_grad: float32 [1024], replicated
- in_weight_grad: float32 [1024, 3, 1024], P(None, None, 'tensor')
- conv_kernel_grad: float32 [3, 1024], P(None, 'tensor')
- out_weight_grad: float32 [1024, 1024], P('tensor')
- ffn_gain_grad: float32 [1024], replicated
- gate_weight_grad: float32 [1024, 4608], P(None, 'tensor')
- up_weight_grad: float32 [1024, 4608], P(None, 'tensor')
- down_weight_grad: float32 [4608, 1024], P('tensor')
Inputs may be any that keep to these rules, and one draw needn't show every extreme that they name: `lengths`: each slot holds one sequence at positions 0 to its length - 1; some slot has length 1024 and some 1024 // 4.
All inputs are finite; a program needn't handle non-finite values.
Results may differ from a plain program's by a relative error of at most 0.022.
Values may be sent and summed in bfloat16 or wider, within the bound.
A program may use at most 256 MiB of HBM per device.

v0:
```python
import functools

import jax
import jax.numpy as jnp
from jax import lax
from jax.experimental import pallas as pl
from jax.experimental.pallas import tpu as pltpu
from jax.sharding import PartitionSpec as P

KERNEL = 3


eps = 1e-05


def rms_forward(values, gain_values):
    inverse = lax.rsqrt(jnp.mean(values * values, axis=-1, keepdims=True) + eps)
    return (values * inverse * gain_values, inverse)


def rms_backward(values, inverse, gain_values, upstream):
    weighted = upstream * gain_values
    gain_part = jnp.sum(upstream * values * inverse, axis=0)
    through = inverse * weighted - values * inverse**3 * jnp.mean(
        weighted * values, axis=-1, keepdims=True
    )
    return (through, gain_part)


def local(
    block_input,
    mixer_gain,
    in_weight,
    conv_kernel,
    out_weight,
    ffn_gain,
    gate_weight,
    up_weight,
    down_weight,
    output_grad,
    lengths,
):
    local_rows = block_input.shape[0]
    model_width = block_input.shape[1]
    channels = in_weight.shape[2]
    slot_count = lengths.shape[0]
    source = block_input.astype(jnp.float32)
    normed_one, inverse_one = rms_forward(source, mixer_gain)
    gathered_one = lax.all_gather(normed_one.astype(jnp.bfloat16), "tensor", axis=0, tiled=True)
    group_rows = gathered_one.shape[0]
    slot_length = group_rows // slot_count
    in_flat = in_weight.reshape(model_width, 3 * channels)
    projected = jnp.dot(gathered_one, in_flat, preferred_element_type=jnp.float32).reshape(
        group_rows, 3, channels
    )
    b_part = projected[:, 0]
    c_part = projected[:, 1]
    x_part = projected[:, 2]
    mixed = (b_part * x_part).reshape(slot_count, slot_length, channels)
    kernel_values = conv_kernel.astype(jnp.float32)
    padded = jnp.pad(mixed, ((0, 0), (KERNEL - 1, 0), (0, 0)))
    convolved = jnp.zeros_like(mixed)
    for offset in range(KERNEL):
        convolved = convolved + kernel_values[offset] * padded[:, offset : offset + slot_length]
    convolved = convolved.reshape(group_rows, channels)
    gated = (c_part * convolved).astype(jnp.bfloat16)
    hidden = source + lax.psum_scatter(
        jnp.dot(gated, out_weight, preferred_element_type=jnp.float32).astype(jnp.bfloat16),
        "tensor",
        scatter_dimension=0,
        tiled=True,
    ).astype(jnp.float32)
    normed_two, inverse_two = rms_forward(hidden, ffn_gain)
    gathered_two = lax.all_gather(normed_two.astype(jnp.bfloat16), "tensor", axis=0, tiled=True)
    gate_value = jnp.dot(gathered_two, gate_weight, preferred_element_type=jnp.float32)
    up_value = jnp.dot(gathered_two, up_weight, preferred_element_type=jnp.float32)
    sigmoid_gate = jax.nn.sigmoid(gate_value)
    silu_value = gate_value * sigmoid_gate
    inner_low = (silu_value * up_value).astype(jnp.bfloat16)
    block_output = (
        hidden
        + lax.psum_scatter(
            jnp.dot(inner_low, down_weight, preferred_element_type=jnp.float32).astype(
                jnp.bfloat16
            ),
            "tensor",
            scatter_dimension=0,
            tiled=True,
        ).astype(jnp.float32)
    ).astype(jnp.bfloat16)
    row_index = lax.axis_index("tensor") * local_rows + jnp.arange(local_rows, dtype=jnp.int32)
    slot_of = row_index // slot_length
    position = row_index % slot_length
    matched = (slot_of[:, None] == jnp.arange(slot_count, dtype=jnp.int32)[None, :]) & (
        position[:, None] < lengths[None, :]
    )
    token_mask = jnp.any(matched, axis=1).astype(jnp.float32)
    cotangent = output_grad.astype(jnp.float32) * token_mask[:, None]
    grad_rows = lax.all_gather(cotangent.astype(jnp.bfloat16), "tensor", axis=0, tiled=True)
    inner_grad = jnp.einsum("rd,fd->rf", grad_rows, down_weight, preferred_element_type=jnp.float32)
    down_weight_grad = jnp.einsum(
        "rf,rd->fd", inner_low, grad_rows, preferred_element_type=jnp.float32
    )
    gate_grad = (
        inner_grad * up_value * sigmoid_gate * (1.0 + gate_value * (1.0 - sigmoid_gate))
    ).astype(jnp.bfloat16)
    up_grad = (inner_grad * silu_value).astype(jnp.bfloat16)
    gate_weight_grad = jnp.einsum(
        "rd,rf->df", gathered_two, gate_grad, preferred_element_type=jnp.float32
    )
    up_weight_grad = jnp.einsum(
        "rd,rf->df", gathered_two, up_grad, preferred_element_type=jnp.float32
    )
    from_gate = jnp.einsum("rf,df->rd", gate_grad, gate_weight, preferred_element_type=jnp.float32)
    normed_two_grad = lax.psum_scatter(
        (
            from_gate
            + jnp.einsum("rf,df->rd", up_grad, up_weight, preferred_element_type=jnp.float32)
        ).astype(jnp.bfloat16),
        "tensor",
        scatter_dimension=0,
        tiled=True,
    ).astype(jnp.float32)
    through_two, ffn_gain_part = rms_backward(hidden, inverse_two, ffn_gain, normed_two_grad)
    hidden_grad = cotangent + through_two
    hidden_rows = lax.all_gather(hidden_grad.astype(jnp.bfloat16), "tensor", axis=0, tiled=True)
    gated_grad = jnp.einsum(
        "rd,cd->rc", hidden_rows, out_weight, preferred_element_type=jnp.float32
    )
    out_weight_grad = jnp.einsum(
        "rc,rd->cd", gated, hidden_rows, preferred_element_type=jnp.float32
    )
    c_grad = gated_grad * convolved
    conv_grad = (gated_grad * c_part).reshape(slot_count, slot_length, channels)
    padded_after = jnp.pad(conv_grad, ((0, 0), (0, KERNEL - 1), (0, 0)))
    mixed_grad = jnp.zeros_like(conv_grad)
    kernel_rows = []
    for offset in range(KERNEL):
        shift_start = KERNEL - 1 - offset
        mixed_grad = (
            mixed_grad
            + kernel_values[offset] * padded_after[:, shift_start : shift_start + slot_length]
        )
        kernel_rows.append(
            jnp.sum(conv_grad * padded[:, offset : offset + slot_length], axis=(0, 1))
        )
    conv_kernel_grad = jnp.stack(kernel_rows, axis=0)
    mixed_grad = mixed_grad.reshape(group_rows, channels)
    projected_grad = jnp.stack([mixed_grad * x_part, c_grad, mixed_grad * b_part], axis=1).astype(
        jnp.bfloat16
    )
    in_weight_grad = jnp.einsum(
        "rd,rkc->dkc", gathered_one, projected_grad, preferred_element_type=jnp.float32
    )
    normed_one_grad = lax.psum_scatter(
        jnp.einsum(
            "rkc,dkc->rd", projected_grad, in_weight, preferred_element_type=jnp.float32
        ).astype(jnp.bfloat16),
        "tensor",
        scatter_dimension=0,
        tiled=True,
    ).astype(jnp.float32)
    through_one, mixer_gain_part = rms_backward(source, inverse_one, mixer_gain, normed_one_grad)
    input_grad = (hidden_grad + through_one).astype(jnp.bfloat16)
    (
        in_weight_grad,
        conv_kernel_grad,
        out_weight_grad,
        gate_weight_grad,
        up_weight_grad,
        down_weight_grad,
    ) = (
        lax.psum(in_weight_grad.astype(jnp.bfloat16), "dp").astype(jnp.float32),
        lax.psum(conv_kernel_grad.astype(jnp.bfloat16), "dp").astype(jnp.float32),
        lax.psum(out_weight_grad.astype(jnp.bfloat16), "dp").astype(jnp.float32),
        lax.psum(gate_weight_grad.astype(jnp.bfloat16), "dp").astype(jnp.float32),
        lax.psum(up_weight_grad.astype(jnp.bfloat16), "dp").astype(jnp.float32),
        lax.psum(down_weight_grad.astype(jnp.bfloat16), "dp").astype(jnp.float32),
    )
    mixer_gain_grad, ffn_gain_grad = lax.psum((mixer_gain_part, ffn_gain_part), ("dp", "tensor"))
    return (
        block_output,
        input_grad,
        mixer_gain_grad,
        in_weight_grad,
        conv_kernel_grad,
        out_weight_grad,
        ffn_gain_grad,
        gate_weight_grad,
        up_weight_grad,
        down_weight_grad,
    )


NN = (((1,), (0,)), ((), ()))
NT = (((1,), (1,)), ((), ()))
TN = (((0,), (0,)), ((), ()))
F32 = jnp.float32
BF16 = jnp.bfloat16


def dot(a, b, dims=NN):
    return lax.dot_general(a, b, dims, preferred_element_type=F32)


MESH = pl.DeviceIdType.MESH
TILE = 256
RING = 4
LAG = 2
LAGS = (2, 3, 5, 6)


def enter(devices):
    barrier = pltpu.get_barrier_semaphore()
    for device in devices:
        pl.semaphore_signal(barrier, inc=1, device_id=device, device_id_type=MESH)
    pl.semaphore_wait(barrier, len(devices))


def widen(values):
    return values.astype(F32)


def inverse_rms(values):
    return lax.rsqrt(jnp.mean(values * values, axis=-1, keepdims=True) + eps)


STEP = 768
PASS = 512


def front_kernel(
    lengths, gain_one, gain_two, taps_own, block_input, output_grad, in_own, out_own, gate_w, up_w, down_w,
    taps_out, cot_h, n2_h, inner_h, gg_h, ug_h, n2g_h, out_h, hidden_h, parts_o, parts_p, in_other, out_other, n1_h, gated_h,
    in_w, out_w, src, other, n1, gated, n2, cot, wg, wu, wd, inner, gg, ug, acc1, acc2, part, hid, low1, low2, prev, taps, taps_low,
    load_sem, w_sem, o_sem, p_sem, h_sem, l_sem, x_send, x_recv, send, recv,
):
    rows, width = src.shape
    channels = out_own.shape[0]
    hidden_units = gate_w.shape[1]
    me = lax.axis_index("dp")
    tensor = lax.axis_index("tensor")
    bits = [(me // (1 << k)) % 2 for k in range(3)]
    peers = [me + (1 << k) - (2 << k) * bits[k] for k in range(3)]
    enter([(p, tensor) for p in peers] + [(me, 1 - tensor)])

    def x_copy(src_ref, dst_ref, k):
        return pltpu.make_async_remote_copy(
            src_ref=src_ref, dst_ref=dst_ref, send_sem=x_send.at[k], recv_sem=x_recv.at[k],
            device_id=(me, 1 - tensor), device_id_type=MESH,
        )

    units = [(in_own.at[k], in_w.at[1, k], width) for k in range(3)] + [(out_own, out_w.at[1], channels)]
    routes = [(1, 2, 0), (2, 1, 0), (2, 1, 0), (1, 2, 0)]

    def span(u, s):
        size = units[u][2]
        first, second, last = routes[u]
        if s == 0:
            start = bits[last] * (size // 2) + bits[second] * (size // 4) + bits[first] * (size // 8)
            return pl.ds(pl.multiple_of(start, size // 8), size // 8)
        if s == 1:
            start = bits[last] * (size // 2) + bits[second] * (size // 4)
            return pl.ds(pl.multiple_of(start, size // 4), size // 4)
        return pl.ds(pl.multiple_of(bits[last] * (size // 2), size // 2), size // 2)

    def cross(u):
        return x_copy(units[u][0].at[span(u, 0)], units[u][1].at[span(u, 0)], u)

    def double(u, s):
        at = span(u, s)
        return pltpu.make_async_remote_copy(
            src_ref=units[u][1].at[at], dst_ref=units[u][1].at[at],
            send_sem=send.at[u, s], recv_sem=recv.at[u, s],
            device_id=(peers[routes[u][s]], tensor), device_id_type=MESH,
        )

    blocks = [pl.ds(k * PASS, PASS) for k in range(rows // PASS)]
    taps_copy = x_copy(taps_own, taps_low, 4)
    input_copies = [x_copy(block_input.at[b], other.at[b], 5 + k) for k, b in enumerate(blocks)]
    grad_copies = [
        x_copy(output_grad.at[b], cot.at[pl.ds(rows + k * PASS, PASS)], 5 + len(blocks) + k)
        for k, b in enumerate(blocks)
    ]
    taps_copy.start()
    for u in range(4):
        cross(u).start()
    for copy in input_copies + grad_copies:
        copy.start()

    def load(k, src_ref, dst_ref):
        return pltpu.make_async_copy(src_ref, dst_ref, load_sem.at[k])

    first_load = load(0, block_input, src)
    own_load = load(1, in_own, in_w.at[0])
    out_load = load(2, out_own, out_w.at[0])
    cot_load = load(3, output_grad, cot.at[pl.ds(0, rows)])
    for copy in (first_load, own_load, out_load, cot_load):
        copy.start()

    steps = hidden_units // STEP

    def weights(u):
        at = pl.ds(pl.multiple_of((u % steps) * STEP, STEP), STEP)
        slot = u % 2
        return [
            pltpu.make_async_copy(gate_w.at[:, at], wg.at[slot], w_sem.at[slot, 0]),
            pltpu.make_async_copy(up_w.at[:, at], wu.at[slot], w_sem.at[slot, 1]),
            pltpu.make_async_copy(down_w.at[at], wd.at[slot], w_sem.at[slot, 2]),
        ]

    for copy in weights(0):
        copy.start()
    taps[0] = widen(taps_own[...])
    first_load.wait()

    tiles = rows // TILE

    def tile_at(i, base=0):
        return pl.ds(pl.multiple_of(base + i * TILE, TILE), TILE)

    def normalize(i, carry):
        values = widen(src[tile_at(i), :])
        n1[tile_at(i), :] = (values * inverse_rms(values) * gain_one[...]).astype(BF16)
        return carry

    lax.fori_loop(0, tiles, normalize, 0)
    n1_store = load(4, n1, n1_h)
    n1_store.start()
    own_load.wait()

    row = lax.broadcasted_iota(jnp.int32, (TILE, channels), 0)

    def mix(normed, h):
        b_part, c_part, x_part = [dot(normed, in_w[h, k]) for k in range(3)]
        mixed = b_part * x_part
        last, before = prev[h, 7:8, :], prev[h, 6:7, :]
        one = jnp.where(row == 0, last, pltpu.roll(mixed, 1, 0))
        two = jnp.where(row == 0, before, jnp.where(row == 1, last, pltpu.roll(mixed, 2, 0)))
        prev[h, :, :] = mixed[TILE - 8 :, :]
        convolved = taps[h, 2:3, :] * mixed + taps[h, 1:2, :] * one + taps[h, 0:1, :] * two
        return b_part, c_part, x_part, convolved, c_part * convolved

    def part_store(h, i):
        out = parts_o if h == 0 else parts_p
        return pltpu.make_async_copy(part.at[i % 2], out.at[tile_at(i)], p_sem.at[i % 2])

    def own_half(i, h):
        pieces = mix(n1[tile_at(i), :], h)
        for k in range(4):
            part[i % 2, :, k * channels : (k + 1) * channels] = pieces[k].astype(BF16)
        gated[tile_at(i), h * channels : (h + 1) * channels] = pieces[4].astype(BF16)
        part_store(h, i).start()

    prev[...] = jnp.zeros_like(prev)

    def first_half(i, carry):
        @pl.when(i >= 2)
        def _():
            part_store(0, i - 2).wait()

        own_half(i, 0)
        for u in range(tiles):

            @pl.when(i == u)
            def _(u=u):
                cross(u).wait()
                double(u, 0).start()
                if u >= 2:
                    double(u - 2, 0).wait()
                    double(u - 2, 1).start()

        return carry

    lax.fori_loop(0, tiles, first_half, 0)
    for u in (2, 3):
        part_store(0, u).wait()
        double(u, 0).wait()
        double(u, 1).start()
    taps_copy.wait()
    taps[1] = widen(taps_low[...])
    for u in range(4):
        double(u, 1).wait()
        double(u, 2).start()

    def masked(base, length):
        def one(i, carry):
            at = tile_at(i, base)
            position = lax.broadcasted_iota(jnp.int32, (TILE, width), 0) + i * TILE
            values = widen(cot[at, :])
            cot[at, :] = jnp.where(position < length, values, jnp.zeros_like(values)).astype(BF16)
            return carry

        return one

    own_length = jnp.where(tensor == 0, lengths[0], lengths[1])
    other_length = jnp.where(tensor == 0, lengths[1], lengths[0])
    cot_load.wait()
    lax.fori_loop(0, tiles, masked(0, own_length), 0)
    cot_store = load(5, cot.at[pl.ds(0, rows)], cot_h.at[pl.ds(0, rows)])
    cot_store.start()
    out_load.wait()
    for u in range(4):
        double(u, 2).wait()
    other_stores = [load(6, in_w.at[1], in_other), load(7, out_w.at[1], out_other)]
    for copy in other_stores:
        copy.start()

    def leave_mixer(values, gated_low, at):
        hidden = values + (dot(gated_low[0], out_w[0]) + dot(gated_low[1], out_w[1]))
        n2[at, :] = (hidden * inverse_rms(hidden) * gain_two[...]).astype(BF16)
        return hidden

    def hid_store(i):
        return pltpu.make_async_copy(hid.at[i % 2], hidden_h.at[tile_at(i)], h_sem.at[i % 2])

    def second_half(i, carry):
        @pl.when(i >= 2)
        def _():
            part_store(1, i - 2).wait()
            hid_store(i - 2).wait()

        own_half(i, 1)
        at = tile_at(i)
        both = [gated[at, h * channels : (h + 1) * channels] for h in range(2)]
        hid[i % 2] = leave_mixer(widen(src[at, :]), both, at)
        hid_store(i).start()
        return carry

    lax.fori_loop(0, tiles, second_half, 0)
    for i in (tiles - 2, tiles - 1):
        part_store(1, i).wait()
        hid_store(i).wait()
    gated_store = load(8, gated, gated_h)
    gated_store.start()
    n2_store = load(9, n2.at[pl.ds(0, rows)], n2_h.at[pl.ds(0, rows)])
    n2_store.start()

    def stores(p, step, slot):
        at = pl.ds(pl.multiple_of(p * PASS, PASS), PASS)
        cols = pl.ds(pl.multiple_of(step * STEP, STEP), STEP)
        return [
            pltpu.make_async_copy(buf.at[slot], out.at[at, cols], o_sem.at[slot, k])
            for k, (buf, out) in enumerate(((inner, inner_h), (gg, gg_h), (ug, ug_h)))
        ]

    def low_stores(p):
        at = pl.ds(pl.multiple_of(p * PASS, PASS), PASS)
        return [
            pltpu.make_async_copy(low1, out_h.at[at], l_sem.at[0]),
            pltpu.make_async_copy(low2, n2g_h.at[at], l_sem.at[1]),
        ]

    passes = 2 * rows // PASS

    def ffn_pass(p, carry):
        acc1[...] = jnp.zeros_like(acc1)
        acc2[...] = jnp.zeros_like(acc2)

        def ffn_step(step, carry):
            u = p * steps + step
            slot = u % 2
            for copy in weights(u):
                copy.wait()

            @pl.when(u + 1 < passes * steps)
            def _():
                for copy in weights(u + 1):
                    copy.start()

            @pl.when(u >= 2)
            def _():
                for copy in stores(p, step, slot):
                    copy.wait()

            def front(r):
                at = tile_at(r, p * PASS)
                a, c = n2[at, :], cot[at, :]
                return dot(a, wg[slot]), dot(a, wu[slot]), dot(c, wd[slot], NT)

            count = PASS // TILE
            held = front(0)
            for r in range(count):
                following = front(r + 1) if r + 1 < count else None
                s = pl.ds(r * TILE, TILE)
                g, v, ig = held
                sig = jax.nn.sigmoid(g)
                silu = g * sig
                low = (silu * v).astype(BF16)
                gg_low = (ig * v * (sig + silu * (1.0 - sig))).astype(BF16)
                ug_low = (ig * silu).astype(BF16)
                inner[slot, s, :] = low
                gg[slot, s, :] = gg_low
                ug[slot, s, :] = ug_low
                acc1[s, :] += dot(low, wd[slot])
                acc2[s, :] += dot(gg_low, wg[slot], NT) + dot(ug_low, wu[slot], NT)
                held = following
            for copy in stores(p, step, slot):
                copy.start()
            return carry

        lax.fori_loop(0, steps, ffn_step, 0)

        @pl.when(p > 0)
        def _():
            for copy in low_stores(p):
                copy.wait()

        low1[...] = acc1[...].astype(BF16)
        low2[...] = acc2[...].astype(BF16)
        for copy in low_stores(p):
            copy.start()
        return carry

    n2_other = load(10, n2.at[pl.ds(rows, rows)], n2_h.at[pl.ds(rows, rows)])

    def other_tile(i, carry):
        values = widen(other[tile_at(i), :])
        normed = (values * inverse_rms(values) * gain_one[...]).astype(BF16)
        both = [mix(normed, h)[4].astype(BF16) for h in range(2)]
        leave_mixer(values, both, tile_at(i, rows))
        return carry

    def arrived(p):
        @pl.when(p == passes // 2)
        def _():
            prev[...] = jnp.zeros_like(prev)
            for copy in input_copies:
                copy.wait()
            lax.fori_loop(0, tiles, other_tile, 0)
            n2_other.start()

        per_block = PASS // TILE
        for k, copy in enumerate(grad_copies):

            @pl.when(p == passes // 2 + k)
            def _(k=k, copy=copy):
                copy.wait()
                lax.fori_loop(k * per_block, (k + 1) * per_block, masked(rows, other_length), 0)

    def whole_pass(p, carry):
        arrived(p)
        return ffn_pass(p, carry)

    lax.fori_loop(0, passes, whole_pass, 0)
    cot_other = load(11, cot.at[pl.ds(rows, rows)], cot_h.at[pl.ds(rows, rows)])
    cot_other.start()
    for slot in range(2):
        for copy in stores(0, 0, slot):
            copy.wait()
    for copy in low_stores(0):
        copy.wait()
    taps_out[...] = taps[...]
    for copy in [n1_store, cot_store, gated_store, n2_store, n2_other, cot_other] + other_stores:
        copy.wait()


def front(lengths, gains, taps_own, block_input, output_grad, in_own, out_own, gate_w, up_w, down_w):
    rows, width = block_input.shape
    channels = out_own.shape[0]
    hidden_units = gate_w.shape[1]
    vmem = pl.BlockSpec(memory_space=pltpu.VMEM)
    hbm = pl.BlockSpec(memory_space=pl.ANY)

    def shaped(*shape, kind=BF16):
        return jax.ShapeDtypeStruct(shape, kind)

    both = 2 * rows
    outs = [
        shaped(2, KERNEL, channels, kind=F32),
        shaped(both, width),
        shaped(both, width),
        shaped(both, hidden_units),
        shaped(both, hidden_units),
        shaped(both, hidden_units),
        shaped(both, width),
        shaped(both, width),
        shaped(rows, width, kind=F32),
        shaped(rows, 4 * channels),
        shaped(rows, 4 * channels),
        shaped(KERNEL, width, channels),
        shaped(channels, width),
        shaped(rows, width),
        shaped(rows, 2 * channels),
    ]
    x_count = 5 + 2 * (rows // PASS)
    dma = pltpu.SemaphoreType.DMA
    return pl.pallas_call(
        front_kernel,
        in_specs=[pl.BlockSpec(memory_space=pltpu.SMEM), vmem, vmem, vmem] + [hbm] * 7,
        out_specs=[vmem] + [hbm] * 14,
        out_shape=outs,
        scratch_shapes=[
            pltpu.VMEM((2, KERNEL, width, channels), BF16),
            pltpu.VMEM((2, channels, width), BF16),
            pltpu.VMEM((rows, width), BF16),
            pltpu.VMEM((rows, width), BF16),
            pltpu.VMEM((rows, width), BF16),
            pltpu.VMEM((rows, 2 * channels), BF16),
            pltpu.VMEM((both, width), BF16),
            pltpu.VMEM((both, width), BF16),
            pltpu.VMEM((2, width, STEP), BF16),
            pltpu.VMEM((2, width, STEP), BF16),
            pltpu.VMEM((2, STEP, width), BF16),
            pltpu.VMEM((2, PASS, STEP), BF16),
            pltpu.VMEM((2, PASS, STEP), BF16),
            pltpu.VMEM((2, PASS, STEP), BF16),
            pltpu.VMEM((PASS, width), F32),
            pltpu.VMEM((PASS, width), F32),
            pltpu.VMEM((2, TILE, 4 * channels), BF16),
            pltpu.VMEM((2, TILE, width), F32),
            pltpu.VMEM((PASS, width), BF16),
            pltpu.VMEM((PASS, width), BF16),
            pltpu.VMEM((2, 8, channels), F32),
            pltpu.VMEM((2, KERNEL, channels), F32),
            pltpu.VMEM((KERNEL, channels), BF16),
            dma((12,)),
            dma((2, 3)),
            dma((2, 3)),
            dma((2,)),
            dma((2,)),
            dma((2,)),
            dma((x_count,)),
            dma((x_count,)),
            dma((4, 3)),
            dma((4, 3)),
        ],
        name="front",
        cost_estimate=pl.CostEstimate(
            flops=24 * rows * width * hidden_units, bytes_accessed=40 * hidden_units * width, transcendentals=0
        ),
        compiler_params=pltpu.CompilerParams(
            collective_id=2, has_side_effects=True, vmem_limit_bytes=63 * 2**20
        ),
    )(lengths, *gains, taps_own, block_input, output_grad, in_own, out_own, gate_w, up_w, down_w)


def back_kernel(
    gain_one, gain_two, taps,
    cot_h, n2_h, inner_h, gg_h, ug_h, n2g_h, out_h,
    hidden, source, parts_o, parts_p, in_o, in_p, out_w_o, out_w_p, n1, gated,
    summed, input_grad, block_out, out_recv, small,
    ring, rc, ry, ra, rb, rx, small_recv, cot, n2, operand, in_w, pg, part, hid, ngo, ngr, src, ig, nxt, kacc,
    load_sem, fixed_sem, tile_sem, send, recv, local_sem, x_send, x_recv, small_send, small_rsem,
):
    width = cot.shape[1]
    rows = n1.shape[0]
    channels = out_w_o.shape[0]
    ffn_chunks = 3 * inner_h.shape[1] // TILE
    in_chunks = 3 * channels // TILE
    own_chunks = in_chunks + channels // TILE
    total = ffn_chunks + own_chunks
    half = width // 2

    me = lax.axis_index("dp")
    tensor = lax.axis_index("tensor")
    bits = [(me // (1 << k)) % 2 for k in range(4)]
    peers = [me + (1 << k) - (2 << k) * bits[k] for k in range(4)]
    z = me // 4
    mirror = me + 4 * (3 - 2 * z)
    inner_z = (z == 1) | (z == 2)
    outer_z = (z == 0) | (z == 3)
    enter([(p, tensor) for p in peers] + [(mirror, tensor), (me, 1 - tensor)])

    def peer_copy(src_ref, dst_ref, slot, j, peer):
        return pltpu.make_async_remote_copy(
            src_ref=src_ref, dst_ref=dst_ref, send_sem=send.at[slot, j], recv_sem=recv.at[slot, j],
            device_id=(peer, tensor), device_id_type=MESH,
        )

    def x_copy(src_ref, dst_ref, k):
        return pltpu.make_async_remote_copy(
            src_ref=src_ref, dst_ref=dst_ref, send_sem=x_send.at[k], recv_sem=x_recv.at[k],
            device_id=(me, 1 - tensor), device_id_type=MESH,
        )

    def rows_at(start, size):
        return pl.ds(pl.multiple_of(start, size), size)

    quarter, eighth = half // 2, half // 4
    core_at = rows_at(bits[0] * half, half)
    core_away = rows_at((1 - bits[0]) * half, half)
    y_at = rows_at(bits[1] * quarter, quarter)
    y_away = rows_at((1 - bits[1]) * quarter, quarter)
    z_at = rows_at(bits[1] * quarter + bits[3] * eighth, eighth)
    z_away = rows_at(bits[1] * quarter + (1 - bits[3]) * eighth, eighth)

    def result(j, start, size):
        return summed.at[j, rows_at(start, size)]

    def result_y(j):
        return result(j, bits[0] * half + bits[1] * quarter, quarter)

    def result_z(j, side):
        return result(j, bits[0] * half + bits[1] * quarter + side * eighth, eighth)

    def scatter0(q):
        return peer_copy(ring.at[q % RING, core_away], rc.at[q], 0, q, peers[0])

    def scatter_y(j):
        return peer_copy(rc.at[j, y_away], ry.at[j], 1, j, peers[1])

    def up(j):
        return peer_copy(rc.at[j, y_at], ra.at[j], 2, j, peers[2])

    def across(j):
        return peer_copy(rc.at[j, z_away], rb.at[j], 3, j, mirror)

    def keep(j):
        return pltpu.make_async_copy(rc.at[j, z_at], result_z(j, bits[3]), local_sem.at[j])

    def gather_across(j):
        return peer_copy(rc.at[j, z_at], result_z(j, bits[3]), 4, j, mirror)

    def down_own(j):
        return peer_copy(rc.at[j, z_at], result_z(j, bits[3]), 5, j, peers[2])

    def down_other(j):
        return peer_copy(result_z(j, 1 - bits[3]), result_z(j, 1 - bits[3]), 6, j, peers[2])

    def gather_y(j):
        return peer_copy(result_y(j), result_y(j), 7, j, peers[1])

    def gather_core(j):
        at = result(j, bits[0] * half, half)
        return peer_copy(at, at, 8, j, peers[0])

    def add(j, at, landed):
        rc[j, at, :] = (widen(rc[j, at, :]) + widen(landed[j])).astype(BF16)

    def when(j, also, what):
        inside = (j >= 0) & (j < total)

        @pl.when(inside if also is None else inside & also)
        def _():
            what(j)

    def tick(k):
        def from_y(j):
            scatter_y(j).wait()
            add(j, y_at, ry)

            @pl.when(outer_z)
            def _():
                up(j).start()

        def from_outer(j):
            up(j).wait_recv()
            add(j, y_at, ra)
            across(j).start()

        def from_inner(j):
            across(j).wait()
            add(j, z_at, rb)
            gather_across(j).start()
            down_own(j).start()
            keep(j).start()

        def to_outer(j):
            gather_across(j).wait()
            keep(j).wait()
            down_other(j).start()

        def to_y_again(j):
            @pl.when(inner_z)
            def _():
                down_own(j).wait_send()

            @pl.when(outer_z)
            def _():
                up(j).wait_send()
                down_own(j).wait_recv()
                down_other(j).wait_recv()

            gather_y(j).start()

        when(k, None, from_y)
        when(k - LAGS[0], inner_z, from_outer)
        when(k - LAGS[1], inner_z, from_inner)
        when(k - LAGS[2], inner_z, to_outer)
        when(k - LAGS[3], None, to_y_again)

    def finish(j):
        gather_y(j).wait()
        gather_core(j).start()

    def ticks(low, high):
        def one(k, carry):
            tick(k)
            return carry

        lax.fori_loop(low, high, one, 0)

    def fixed(k, src_ref, dst_ref):
        return pltpu.make_async_copy(src_ref, dst_ref, fixed_sem.at[k])

    first_loads = [fixed(0, cot_h, cot)]
    second_loads = [fixed(1, n2_h, n2)]
    mixer_loads = [fixed(2, in_o, in_w.at[0]), fixed(3, in_p, in_w.at[1])]
    out_loads = [
        fixed(4, out_w_o, cot.at[pl.ds(rows, channels)]),
        fixed(5, out_w_p, cot.at[pl.ds(rows + channels, channels)]),
    ]
    late_loads = [fixed(6, n1, n2.at[pl.ds(0, rows)]), fixed(7, gated, n2.at[pl.ds(rows, rows)])]

    def start(copies):
        for copy in copies:
            copy.start()

    def wait(copies):
        for copy in copies:
            copy.wait()

    groups = (inner_h, gg_h, ug_h)
    per = ffn_chunks // 3

    def operands(group, i, slot):
        cols = pl.ds(pl.multiple_of(i * TILE, TILE), TILE)
        return [pltpu.make_async_copy(groups[group].at[:, cols], operand.at[slot], load_sem.at[slot])]

    start(first_loads)
    start(operands(0, 0, 0))
    start(second_loads)
    start(mixer_loads)

    tiles = rows // TILE

    def n2g_block(i):
        at = (tiles - 1 - i) * TILE
        return x_copy(
            n2g_h.at[pl.ds(pl.multiple_of(rows + at, TILE), TILE)],
            ngr.at[pl.ds(pl.multiple_of(at, TILE), TILE)],
            i,
        )

    for i in range(tiles):
        n2g_block(i).start()
    last_swap = x_copy(out_h.at[pl.ds(rows, rows)], out_recv, tiles + own_chunks)
    last_swap.start()
    wait(first_loads)

    def from_core(q):
        scatter0(q).wait()
        rc[q] = (widen(ring[q % RING, core_at, :]) + widen(rc[q])).astype(BF16)

    def to_y(j):
        from_core(j)
        scatter_y(j).start()

    for group in range(3):
        if group == 1:
            wait(second_loads)
            start(out_loads)

        def compute(i, carry, group=group):
            j = group * per + i
            slot = j % 2
            wait(operands(group, i, slot))

            @pl.when(i + 1 < per)
            def _():
                start(operands(group, i + 1, 1 - slot))

            if group < 2:

                @pl.when(i + 1 == per)
                def _():
                    start(operands(group + 1, 0, 1 - slot))

            left = cot if group == 0 else n2
            ring[j % RING] = dot(left[...], operand[slot], TN).astype(BF16)
            scatter0(j).start()

            @pl.when(j >= LAG)
            def _():
                to_y(j - LAG)

            @pl.when(j >= 10)
            def _():
                tick(j - 10)

            return carry

        lax.fori_loop(0, per, compute, 0)
    start(late_loads)
    for j in range(ffn_chunks - LAG, ffn_chunks):
        to_y(j)
    done = ffn_chunks - 10

    nxt[...] = jnp.zeros_like(nxt)
    kacc[...] = jnp.zeros_like(kacc)
    small[...] = jnp.zeros_like(small)
    wait(mixer_loads)
    wait(out_loads)

    def mixer(i, carry):
        at = pl.ds(pl.multiple_of((tiles - 1 - i) * TILE, TILE), TILE)
        loads = [
            pltpu.make_async_copy(hidden.at[at], hid, tile_sem.at[0]),
            pltpu.make_async_copy(n2g_h.at[at], ngo, tile_sem.at[1]),
            pltpu.make_async_copy(source.at[at], src, tile_sem.at[2]),
            pltpu.make_async_copy(parts_o.at[at], part.at[0], tile_sem.at[3]),
            pltpu.make_async_copy(parts_p.at[at], part.at[1], tile_sem.at[4]),
        ]
        start(loads)
        n2g_block(i).wait()
        wait(loads)
        upstream = widen(ngo[...]) + widen(ngr[at, :])
        values = hid[...]
        inverse = lax.rsqrt(jnp.mean(values * values, axis=-1, keepdims=True) + eps)
        weighted = upstream * gain_two[...]
        scaled = values * inverse
        small[1:2, :] += jnp.sum(upstream * scaled, axis=0, keepdims=True)
        along = jnp.mean(weighted * scaled, axis=-1, keepdims=True)
        grad = widen(cot[at, :]) + inverse * (weighted - scaled * along)
        grad_low = grad.astype(BF16)
        cot[at, :] = grad_low
        row = lax.broadcasted_iota(jnp.int32, (TILE, channels), 0)
        upstream_one = jnp.zeros((TILE, width), F32)
        for h in range(2):
            out_w = cot[pl.ds(rows + h * channels, channels), :]
            gated_grad = dot(grad_low, out_w, NT)
            b_part = widen(part[h, :, 0:channels])
            c_part = widen(part[h, :, channels : 2 * channels])
            x_part = widen(part[h, :, 2 * channels : 3 * channels])
            convolved = widen(part[h, :, 3 * channels : 4 * channels])
            conv_grad = gated_grad * c_part
            one = jnp.where(row == TILE - 1, nxt[h, 0:1, :], pltpu.roll(conv_grad, TILE - 1, 0))
            two = jnp.where(
                row == TILE - 1,
                nxt[h, 1:2, :],
                jnp.where(row == TILE - 2, nxt[h, 0:1, :], pltpu.roll(conv_grad, TILE - 2, 0)),
            )
            nxt[h, 0:2, :] = conv_grad[0:2, :]
            mixed_grad = taps[h, 2:3, :] * conv_grad + taps[h, 1:2, :] * one + taps[h, 0:1, :] * two
            mixed = b_part * x_part
            kacc[h, 0:1, :] += jnp.sum(mixed * two, axis=0, keepdims=True)
            kacc[h, 1:2, :] += jnp.sum(mixed * one, axis=0, keepdims=True)
            kacc[h, 2:3, :] += jnp.sum(mixed * conv_grad, axis=0, keepdims=True)
            for k, piece_grad in enumerate((mixed_grad * x_part, gated_grad * convolved, mixed_grad * b_part)):
                low = piece_grad.astype(BF16)
                pg[h, at, k * channels : (k + 1) * channels] = low
                upstream_one = upstream_one + dot(low, in_w[h, k], NT)
        values_one = widen(src[...])
        inverse_one = lax.rsqrt(jnp.mean(values_one * values_one, axis=-1, keepdims=True) + eps)
        weighted_one = upstream_one * gain_one[...]
        scaled_one = values_one * inverse_one
        small[0:1, :] += jnp.sum(upstream_one * scaled_one, axis=0, keepdims=True)
        along_one = jnp.mean(weighted_one * scaled_one, axis=-1, keepdims=True)
        ig[...] = (grad + inverse_one * (weighted_one - scaled_one * along_one)).astype(BF16)
        store = pltpu.make_async_copy(ig, input_grad.at[at], tile_sem.at[5])
        store.start()
        store.wait()
        return carry

    lax.fori_loop(0, tiles, mixer, 0)
    wait(late_loads)

    def piece(h, m_in, m_out):
        if m_in is not None:
            cols = pl.ds(pl.multiple_of(m_in * TILE, TILE), TILE)
            return dot(n2[0:rows, :], pg[h, :, cols], TN)
        cols = pl.ds(pl.multiple_of(h * channels + m_out * TILE, TILE), TILE)
        return dot(cot[0:rows, :], n2[rows : 2 * rows, cols], TN)

    def cross(m):
        return x_copy(rc.at[total + m], rx.at[m], tiles + m)

    def after_core(h, m):
        if h == 1:
            from_core(total + m)
            cross(m).start()
        else:
            from_core(ffn_chunks + m)

    for h in (1, 0):
        base = total if h == 1 else ffn_chunks

        def in_piece(m, carry, h=h, base=base):
            q = base + m
            ring[q % RING] = piece(h, m, None).astype(BF16)
            scatter0(q).start()

            @pl.when(m >= LAG)
            def _():
                after_core(h, m - LAG)

            k = done + m + (in_chunks if h == 0 else 0)

            @pl.when(k < ffn_chunks)
            def _():
                tick(k)

            return carry

        lax.fori_loop(0, in_chunks, in_piece, 0)
        for m in range(in_chunks, own_chunks):
            ring[(base + m) % RING] = piece(h, None, m - in_chunks).astype(BF16)
            scatter0(base + m).start()
            after_core(h, m - LAG)
        for m in range(own_chunks - LAG, own_chunks):
            after_core(h, m)
    for h in range(2):
        cols = pl.ds(pl.multiple_of(channels * (tensor + h - 2 * tensor * h), channels), channels)
        small[2:5, cols] = kacc[h, 0:3, :]

    def small_copy(k):
        device = (peers[k], tensor) if k < 4 else (me, 1 - tensor)
        return pltpu.make_async_remote_copy(
            src_ref=small, dst_ref=small_recv.at[k], send_sem=small_send.at[k], recv_sem=small_rsem.at[k],
            device_id=device, device_id_type=MESH,
        )

    def crossed(m, carry):
        cross(m).wait()
        j = ffn_chunks + m
        rc[j] = (widen(rc[j]) + widen(rx[m])).astype(BF16)
        scatter_y(j).start()
        finish(m)
        return carry

    lax.fori_loop(0, own_chunks, crossed, 0)
    for k in range(5):
        small_copy(k).start()
        small_copy(k).wait()
        small[...] = small[...] + small_recv[k]

    last_swap.wait()

    def leave(i, carry):
        at = pl.ds(pl.multiple_of(i * TILE, TILE), TILE)
        loads = [
            pltpu.make_async_copy(hidden.at[at], hid, tile_sem.at[0]),
            pltpu.make_async_copy(out_h.at[at], ngo, tile_sem.at[1]),
            pltpu.make_async_copy(out_recv.at[at], src, tile_sem.at[2]),
        ]
        start(loads)
        wait(loads)
        ig[...] = (hid[...] + (widen(ngo[...]) + widen(src[...]))).astype(BF16)
        store = pltpu.make_async_copy(ig, block_out.at[at], tile_sem.at[5])
        store.start()
        store.wait()
        return carry

    lax.fori_loop(0, tiles, leave, 0)

    last_tick = total + LAGS[3]
    turn = 2 * ffn_chunks - own_chunks - LAGS[3] - 3

    def drain_two(k, carry):
        tick(k)
        finish(own_chunks + 2 * (k - ffn_chunks))
        finish(own_chunks + 2 * (k - ffn_chunks) + 1)
        return carry

    def drain_one(k, carry):
        tick(k)
        finish(k - LAGS[3] - 3)
        return carry

    def drain(j, carry):
        finish(j)
        return carry

    lax.fori_loop(ffn_chunks, turn, drain_two, 0)
    lax.fori_loop(turn, last_tick, drain_one, 0)
    lax.fori_loop(last_tick - LAGS[3] - 3, total, drain, 0)

    def arrive(j, carry):
        gather_core(j).wait()

        @pl.when(inner_z)
        def _():
            down_other(j).wait_send()

        return carry

    lax.fori_loop(0, total, arrive, 0)


def back(gains, taps, arrays, rows, width, hidden, channels):
    ffn_chunks = 3 * hidden // TILE
    own_chunks = 4 * channels // TILE
    total = ffn_chunks + own_chunks
    half = width // 2
    vmem = pl.BlockSpec(memory_space=pltpu.VMEM)
    hbm = pl.BlockSpec(memory_space=pl.ANY)

    def buffer(count, size):
        return pltpu.VMEM((count, size, TILE), BF16)

    return pl.pallas_call(
        back_kernel,
        in_specs=[vmem, vmem, vmem] + [hbm] * len(arrays),
        out_specs=[hbm, hbm, hbm, hbm, vmem],
        out_shape=[
            jax.ShapeDtypeStruct((total, width, TILE), BF16),
            jax.ShapeDtypeStruct((rows, width), BF16),
            jax.ShapeDtypeStruct((rows, width), BF16),
            jax.ShapeDtypeStruct((rows, width), BF16),
            jax.ShapeDtypeStruct((8, width), F32),
        ],
        scratch_shapes=[
            buffer(RING, width),
            buffer(total + own_chunks, half),
            buffer(total, half // 2),
            buffer(total, half // 2),
            buffer(total, half // 4),
            buffer(own_chunks, half),
            pltpu.VMEM((5, 8, width), F32),
            pltpu.VMEM((2 * rows, width), BF16),
            pltpu.VMEM((2 * rows, width), BF16),
            buffer(2, 2 * rows),
            pltpu.VMEM((2, 3, width, channels), BF16),
            pltpu.VMEM((2, rows, 3 * channels), BF16),
            pltpu.VMEM((2, TILE, 4 * channels), BF16),
            pltpu.VMEM((TILE, width), F32),
            pltpu.VMEM((TILE, width), BF16),
            pltpu.VMEM((rows, width), BF16),
            pltpu.VMEM((TILE, width), BF16),
            pltpu.VMEM((TILE, width), BF16),
            pltpu.VMEM((2, 8, channels), F32),
            pltpu.VMEM((2, 8, channels), F32),
            pltpu.SemaphoreType.DMA((2,)),
            pltpu.SemaphoreType.DMA((8,)),
            pltpu.SemaphoreType.DMA((6,)),
            pltpu.SemaphoreType.DMA((9, total + own_chunks)),
            pltpu.SemaphoreType.DMA((9, total + own_chunks)),
            pltpu.SemaphoreType.DMA((total,)),
            pltpu.SemaphoreType.DMA((rows // TILE + own_chunks + 1,)),
            pltpu.SemaphoreType.DMA((rows // TILE + own_chunks + 1,)),
            pltpu.SemaphoreType.DMA((5,)),
            pltpu.SemaphoreType.DMA((5,)),
        ],
        name="back",
        cost_estimate=pl.CostEstimate(
            flops=12 * rows * width * hidden + 32 * rows * width * channels,
            bytes_accessed=20 * hidden * width,
            transcendentals=0,
        ),
        compiler_params=pltpu.CompilerParams(
            collective_id=1, has_side_effects=True, vmem_limit_bytes=63 * 2**20
        ),
    )(*gains, taps, *arrays)


def finish_kernel(
    summed, block_in, grad_in, down, gate, up, in_grad, out, block_out, grad_out, buf, wide, turned, held, sem_in, sem_out, sem_keep
):
    width = summed.shape[1]
    most = buf.shape[1]
    hidden_units, channels = down.shape[0], out.shape[0]
    per, halves = hidden_units // TILE, channels // TILE
    fetches = [
        pltpu.make_async_copy(block_in, held.at[0], sem_keep.at[0]),
        pltpu.make_async_copy(grad_in, held.at[1], sem_keep.at[1]),
    ]
    keeps = [
        pltpu.make_async_copy(held.at[0], block_out, sem_keep.at[2]),
        pltpu.make_async_copy(held.at[1], grad_out, sem_keep.at[3]),
    ]
    jobs = []
    for group, target in ((1, gate), (0, down), (2, up)):
        for i in range(0, per, most):
            at = pl.ds(i * TILE, most * TILE)
            place = target.at[at] if group == 0 else target.at[:, at]
            jobs.append((group * per + i, most, group == 0, place))
    jobs.append((3 * per + KERNEL * halves, halves, True, out))
    for k in range(KERNEL):
        jobs.append((3 * per + k * halves, halves, False, in_grad.at[k]))

    def load(n):
        first, count = jobs[n][0], jobs[n][1]
        return pltpu.make_async_copy(
            summed.at[pl.ds(first, count)], buf.at[n % 2, pl.ds(0, count)], sem_in.at[n % 2]
        )

    def store(n):
        _, count, turn, place = jobs[n]
        size = count * TILE
        source = turned.at[n % 2, pl.ds(0, size)] if turn else wide.at[n % 2, :, pl.ds(0, size)]
        return pltpu.make_async_copy(source, place, sem_out.at[n % 2])

    load(0).start()
    load(1).start()
    for n, (_, count, turn, _) in enumerate(jobs):
        load(n).wait()
        if n >= 2:
            store(n - 2).wait()
        slot = n % 2
        for k in range(count):
            at = slice(k * TILE, (k + 1) * TILE)
            if turn:
                turned[slot, at, :] = widen(buf[slot, k]).T
            else:
                wide[slot, :, at] = widen(buf[slot, k])
        store(n).start()
        if n + 2 < len(jobs):
            load(n + 2).start()
        if n == 1:
            for copy in fetches:
                copy.start()
        if n == 4:
            for fetch, copy in zip(fetches, keeps):
                fetch.wait()
                copy.start()
    for n in (len(jobs) - 2, len(jobs) - 1):
        store(n).wait()
    for copy in keeps:
        copy.wait()


def finish_grads(summed, block_output, input_grad, hidden_units, channels):
    width = summed.shape[1]
    hbm = pl.BlockSpec(memory_space=pl.ANY)
    low = jax.ShapeDtypeStruct(block_output.shape, BF16)
    return pl.pallas_call(
        finish_kernel,
        in_specs=[hbm] * 3,
        out_specs=[hbm] * 7,
        out_shape=[
            jax.ShapeDtypeStruct((hidden_units, width), F32),
            jax.ShapeDtypeStruct((width, hidden_units), F32),
            jax.ShapeDtypeStruct((width, hidden_units), F32),
            jax.ShapeDtypeStruct((KERNEL, width, channels), F32),
            jax.ShapeDtypeStruct((channels, width), F32),
            low,
            low,
        ],
        scratch_shapes=[
            pltpu.VMEM((2, STEP // TILE, width, TILE), BF16),
            pltpu.VMEM((2, width, STEP), F32),
            pltpu.VMEM((2, STEP, width), F32),
            pltpu.VMEM((2,) + block_output.shape, BF16),
            pltpu.SemaphoreType.DMA((2,)),
            pltpu.SemaphoreType.DMA((2,)),
            pltpu.SemaphoreType.DMA((4,)),
        ],
        name="finish_grads",
        compiler_params=pltpu.CompilerParams(vmem_limit_bytes=63 * 2**20),
    )(summed, block_output, input_grad)


def fast(
    block_input,
    mixer_gain,
    in_weight,
    conv_kernel,
    out_weight,
    ffn_gain,
    gate_weight,
    up_weight,
    down_weight,
    output_grad,
    lengths,
):
    rows, width = block_input.shape
    channels, hidden_units = out_weight.shape[0], gate_weight.shape[1]
    me = lax.axis_index("tensor")
    gains = (mixer_gain[None], ffn_gain[None])
    in_parts = jnp.transpose(in_weight, (1, 0, 2))
    taps, cot, n2, inner, gg, ug, n2g, out, hidden, parts_o, parts_p, in_other, out_other, n1, gated = front(
        lengths,
        gains,
        conv_kernel,
        block_input,
        output_grad,
        in_parts,
        out_weight,
        gate_weight,
        up_weight,
        down_weight,
    )
    arrays = (cot, n2, inner, gg, ug, n2g, out, hidden, block_input, parts_o, parts_p)
    arrays += (in_parts, in_other, out_weight, out_other, n1, gated)
    summed, input_grad, block_output, _, small = back(gains, taps, arrays, rows, width, hidden_units, channels)
    down_grad, gate_grad, up_grad, in_grad, out_grad, block_output, input_grad = finish_grads(
        summed, block_output, input_grad, hidden_units, channels
    )
    conv_kernel_grad = lax.dynamic_slice_in_dim(small[2 : 2 + KERNEL], me * channels, channels, axis=1)
    return (
        block_output,
        input_grad,
        small[0],
        jnp.transpose(in_grad, (1, 0, 2)),
        conv_kernel_grad,
        out_grad,
        small[1],
        gate_grad,
        up_grad,
        down_grad,
    )


def solution(mesh):
    def step(*args):
        rows, slots = args[0].shape[0], args[10].shape[0]
        one_slot_each = mesh.shape["tensor"] == 2 and mesh.shape["dp"] == 16 and slots == 2 and rows == 4 * TILE
        return (fast if one_slot_each else local)(*args)

    return jax.shard_map(
        step,
        mesh=mesh,
        in_specs=(
            P(("dp", "tensor"), None),
            P(),
            P(None, None, "tensor"),
            P(None, "tensor"),
            P("tensor", None),
            P(),
            P(None, "tensor"),
            P(None, "tensor"),
            P("tensor", None),
            P(("dp", "tensor"), None),
            P("dp"),
        ),
        out_specs=(
            P(("dp", "tensor"), None),
            P(("dp", "tensor"), None),
            P(),
            P(None, None, "tensor"),
            P(None, "tensor"),
            P("tensor", None),
            P(),
            P(None, "tensor"),
            P(None, "tensor"),
            P("tensor", None),
        ),
        check_vma=False,
    )
```

profile of v0, /device:TPU:0, one launch (start us, length us, event | category | flops | bytes accessed | tf_op | source)
XLA Modules:
  0.0 393.3 jit_solution(9158975143271226660)
XLA Ops:
  0.6 127.8 %front.1 = (f32[2,3,512]{2,1,0:T(4,128)}, bf16[2048,1024]{1,0:T(8,128)(2,1)}, bf16[2048,1024]{1,0:T(8,128)(2,1)}, bf16[2048,2304]{1,0:T(8,128)(2,1)}, bf16[2048,...) custom-call(s32[2]{0:T(128)} %lengths.1, ...), custom_call_target="tpu_custom_call" | custom-call | flops 57982058496 | bytes 94371840 | tf_op jit(solution)/shard_map/front/pallas_call | solution.py:588
  128.4 241.0 %back.1 = (bf16[35,1024,256]{2,1,0:T(8,128)(2,1)}, bf16[1024,1024]{1,0:T(8,128)(2,1)}, bf16[1024,1024]{1,0:T(8,128)(2,1)}, bf16[1024,1024]{1,0:T(8,128)(2,1)}, f32[8,1024]{1,0:T(8,128)}) custom-call(f32[1,1024]{1,0:T(1,128)} %bitcast.12, f32[1,1024]{1,0:T(1,128)} %bitcast.14, f32[2,3,512]{2,1,0:T(4,128)} %get-tuple-element.36.taps, ...), custom_call_target="tpu_custom_call" | custom-call | flops 46170898432 | bytes 47185920 | tf_op jit(solution)/shard_map/back/pallas_call | solution.py:1092
  369.4 0.0 copy-start
  369.4 22.6 %finish_grads.1 = (f32[2304,1024]{1,0:T(8,128)}, f32[1024,2304]{1,0:T(8,128)}, f32[1024,2304]{1,0:T(8,128)}, f32[3,1024,512]{2,1,0:T(8,128)}, f32[512,1024]{1,0:...) custom-call(bf16[35,1024,256]{2,1,0:T(8,128)(2,1)} %get-tuple-element.51.summed, ...), custom_call_target="tpu_custom_call" | custom-call | tf_op jit(solution)/shard_map/finish_grads/pallas_call | solution.py:1217
  392.1 0.0 copy-done
  392.1 0.6 constant_dynamic-slice_fusion
  392.7 0.6 fusion
  (1 shorter events, 0.0 us)
Async XLA Ops:
  369.4 22.7 %copy-start = (f32[8,1024]{1,0:T(8,128)S(1)}, f32[8,1024]{1,0:T(8,128)}, u32[]{:S(2)}) copy-start(f32[8,1024]{1,0:T(8,128)} %get-tuple-element.56) | copy-start | bytes 98308
where the time goes:
time: 394 us; the launch traced here: 393 us
  Pallas kernels  391 us (99%)
    pallas_call x1, Pallas kernels, back(): pl.pallas_call(back_kernel, in_specs=[vmem, vmem, vmem] + [hbm] * len(arr...  241 us
    pallas_call x1, Pallas kernels, front(): pl.pallas_call(front_kernel, in_specs=[pl.BlockSpec(memory_space=pltpu.SM...  128 us
    pallas_call x1, Pallas kernels, finish_grads(): pl.pallas_call(finish_kernel, in_specs=[hbm] * 3, out_specs=[hbm] * 7, ou...  22.6 us

commit v1 on v0

--- a/solution.py
+++ b/solution.py
@@ -1020,10 +1020,30 @@
         return carry
 
     lax.fori_loop(0, own_chunks, crossed, 0)
+    last_tick = total + LAGS[3]
+    turn = 2 * ffn_chunks - own_chunks - LAGS[3] - 3
+
+    def drain_two(k, carry):
+        tick(k)
+        finish(own_chunks + 2 * (k - ffn_chunks))
+        finish(own_chunks + 2 * (k - ffn_chunks) + 1)
+        return carry
+
+    def drain_one(k, carry):
+        tick(k)
+        finish(k - LAGS[3] - 3)
+        return carry
+
+    def drain(j, carry):
+        finish(j)
+        return carry
+
+    lax.fori_loop(ffn_chunks, turn, drain_two, 0)
     for k in range(5):
         small_copy(k).start()
         small_copy(k).wait()
         small[...] = small[...] + small_recv[k]
+    lax.fori_loop(turn, last_tick, drain_one, 0)
 
     last_swap.wait()
 
@@ -1044,26 +1064,6 @@
 
     lax.fori_loop(0, tiles, leave, 0)
 
-    last_tick = total + LAGS[3]
-    turn = 2 * ffn_chunks - own_chunks - LAGS[3] - 3
-
-    def drain_two(k, carry):
-        tick(k)
-        finish(own_chunks + 2 * (k - ffn_chunks))
-        finish(own_chunks + 2 * (k - ffn_chunks) + 1)
-        return carry
-
-    def drain_one(k, carry):
-        tick(k)
-        finish(k - LAGS[3] - 3)
-        return carry
-
-    def drain(j, carry):
-        finish(j)
-        return carry
-
-    lax.fori_loop(ffn_chunks, turn, drain_two, 0)
-    lax.fori_loop(turn, last_tick, drain_one, 0)
     lax.fori_loop(last_tick - LAGS[3] - 3, total, drain, 0)
 
     def arrive(j, carry):

time: 394 us -> 390 us (0.990)
  Pallas kernels: 391 us -> 387 us
    pallas_call x1, Pallas kernels: 241 us -> 237 us  [back(): pl.pallas_call(back_kernel, in_specs=[vmem, vmem, vmem] + [hbm] * len(arr...]
where the time goes in v1:
time: 390 us; the launch traced here: 389 us
  Pallas kernels  387 us (99%)
    pallas_call x1, Pallas kernels, back(): pl.pallas_call(back_kernel, in_specs=[vmem, vmem, vmem] + [hbm] * len(arr...  237 us
    pallas_call x1, Pallas kernels, front(): pl.pallas_call(front_kernel, in_specs=[pl.BlockSpec(memory_space=pltpu.SM...  128 us
    pallas_call x1, Pallas kernels, finish_grads(): pl.pallas_call(finish_kernel, in_specs=[hbm] * 3, out_specs=[hbm] * 7, ou...  22.6 us

profile of v1, /device:TPU:0, one launch (start us, length us, event | category | flops | bytes accessed | tf_op | source)
XLA Modules:
  0.0 389.2 jit_solution(5919857474357666215)
XLA Ops:
  0.6 127.8 %front.1 = (f32[2,3,512]{2,1,0:T(4,128)}, bf16[2048,1024]{1,0:T(8,128)(2,1)}, bf16[2048,1024]{1,0:T(8,128)(2,1)}, bf16[2048,2304]{1,0:T(8,128)(2,1)}, bf16[2048,...) custom-call(s32[2]{0:T(128)} %lengths.1, ...), custom_call_target="tpu_custom_call" | custom-call | flops 57982058496 | bytes 94371840 | tf_op jit(solution)/shard_map/front/pallas_call | solution.py:588
  128.4 236.9 %back.1 = (bf16[35,1024,256]{2,1,0:T(8,128)(2,1)}, bf16[1024,1024]{1,0:T(8,128)(2,1)}, bf16[1024,1024]{1,0:T(8,128)(2,1)}, bf16[1024,1024]{1,0:T(8,128)(2,1)}, f32[8,1024]{1,0:T(8,128)}) custom-call(f32[1,1024]{1,0:T(1,128)} %bitcast.12, f32[1,1024]{1,0:T(1,128)} %bitcast.14, f32[2,3,512]{2,1,0:T(4,128)} %get-tuple-element.36.taps, ...), custom_call_target="tpu_custom_call" | custom-call | flops 46170898432 | bytes 47185920 | tf_op jit(solution)/shard_map/back/pallas_call | solution.py:1092
  365.3 0.0 copy-start
  365.3 22.6 %finish_grads.1 = (f32[2304,1024]{1,0:T(8,128)}, f32[1024,2304]{1,0:T(8,128)}, f32[1024,2304]{1,0:T(8,128)}, f32[3,1024,512]{2,1,0:T(8,128)}, f32[512,1024]{1,0:...) custom-call(bf16[35,1024,256]{2,1,0:T(8,128)(2,1)} %get-tuple-element.51.summed, ...), custom_call_target="tpu_custom_call" | custom-call | tf_op jit(solution)/shard_map/finish_grads/pallas_call | solution.py:1217
  388.0 0.0 copy-done
  388.0 0.6 constant_dynamic-slice_fusion
  388.6 0.6 fusion
  (1 shorter events, 0.0 us)
Async XLA Ops:
  365.3 22.7 %copy-start = (f32[8,1024]{1,0:T(8,128)S(1)}, f32[8,1024]{1,0:T(8,128)}, u32[]{:S(2)}) copy-start(f32[8,1024]{1,0:T(8,128)} %get-tuple-element.56) | copy-start | bytes 98308
